TPU v7x, 32 devices: a whole 2x2x4 slice. The times are simulated.
32 devices in a mesh: seq: 2 (over x), dp: 16 (over z, y, core).
Axes of the slice: x: 2, y: 2, z: 4, core: 2. Of those that a mesh axis runs over, the one named last changes fastest.
Arguments:
- tokens: bfloat16 [16, 2048, 768], P('dp', 'seq'), may hold values from -6 to 6
- lengths: int32 [16], P('dp'), may hold values from 1024 to 2048, as said below
- w_qkv: bfloat16 [768, 2304], P('dp'), may hold values from -0.21875 to 0.21875
- bias_qv: bfloat16 [1536], P('dp'), may hold values from -3 to 3
- w_out: bfloat16 [768, 768], P('dp'), may hold values from -4 to 4
- bias_out: bfloat16 [768], P('dp'), may hold values from -3 to 3
- w_up: bfloat16 [768, 3072], P('dp'), may hold values from -0.21875 to 0.21875
- bias_up: bfloat16 [3072], P('dp'), may hold values from -3 to 3
- w_down: bfloat16 [3072, 768], P('dp'), may hold values from -0.109375 to 0.109375
- bias_down: bfloat16 [768], P('dp'), may hold values from -3 to 3
- gain_attn: bfloat16 [768], P('dp'), may hold values from 0.099609375 to 1.8984375
- shift_attn: bfloat16 [768], P('dp'), may hold values from -3 to 3
- gain_ffn: bfloat16 [768], P('dp'), may hold values from 0.099609375 to 1.8984375
- shift_ffn: bfloat16 [768], P('dp'), may hold values from -3 to 3
- cotangent: bfloat16 [16, 2048, 768], P('dp', 'seq'), may hold values from -6 to 6
Outputs:
- result: bfloat16 [16, 2048, 768], P('dp', 'seq')
- grad_tokens: float32 [16, 2048, 768], P('dp', 'seq')
- grad_w_qkv: float32 [768, 2304], P('dp')
- grad_bias_qv: float32 [1536], P('dp')
- grad_w_out: float32 [768, 768], P('dp')
- grad_bias_out: float32 [768], P('dp')
- grad_w_up: float32 [768, 3072], P('dp')
- grad_bias_up: float32 [3072], P('dp')
- grad_w_down: float32 [3072, 768], P('dp')
- grad_bias_down: float32 [768], P('dp')
- grad_gain_attn: float32 [768], P('dp')
- grad_shift_attn: float32 [768], P('dp')
- grad_gain_ffn: float32 [768], P('dp')
- grad_shift_ffn: float32 [768], P('dp')
Inputs may be any that keep to these rules, and one draw needn't show every extreme that they name: `lengths`: in every draw some sequence is exactly 2048 long and some other exactly 1024.
All inputs are finite; a program needn't handle non-finite values.
Results may differ from a plain program's by a relative error of at most 0.015.
Values may be sent and summed in bfloat16 or wider, within the bound.
A program may use at most 256 MiB of HBM per device.

v0:
```python
import jax
import jax.numpy as jnp
from jax import lax
from jax.sharding import PartitionSpec as P

HEADS = 12
HD = 64
EPS = 1e-05


def layer_norm(values, gain, offset):
    center = jnp.mean(values, axis=-1, keepdims=True)
    shifted = values - center
    spread = jnp.mean(shifted * shifted, axis=-1, keepdims=True)
    return shifted * lax.rsqrt(spread + EPS) * gain + offset


def gelu_exact(values):
    return 0.5 * values * (1.0 + lax.erf(values * 0.7071067811865476))


def matmul(left, right):
    return jnp.dot(left, right, preferred_element_type=jnp.float32)


def matmul_tn(left, right):
    return lax.dot_general(
        left, right, (((0,), (0,)), ((), ())), preferred_element_type=jnp.float32
    )


def matmul_nt(left, right):
    return lax.dot_general(
        left, right, (((1,), (1,)), ((), ())), preferred_element_type=jnp.float32
    )


def column_sum(values):
    return jnp.sum(values.astype(jnp.float32), axis=0)


def local(
    tokens,
    lengths,
    w_qkv,
    bias_qv,
    w_out,
    bias_out,
    w_up,
    bias_up,
    w_down,
    bias_down,
    gain_attn,
    shift_attn,
    gain_ffn,
    shift_ffn,
    cotangent,
):
    inputs = tokens[0]
    rows_dev = inputs.shape[0]
    width = inputs.shape[1]
    groups = lax.axis_size("seq")
    slot_rows = rows_dev * groups
    head_width = width // groups
    heads_dev = HEADS // groups
    scale = HD ** (-0.5)
    (
        full_qkv,
        full_bqv,
        full_wout,
        full_bout,
        full_wup,
        full_bup,
        full_wdown,
        full_bdown,
        full_gain_one,
        full_shift_one,
        full_gain_two,
        full_shift_two,
    ) = (
        lax.all_gather(w_qkv, "dp", axis=0, tiled=True),
        lax.all_gather(bias_qv, "dp", axis=0, tiled=True),
        lax.all_gather(w_out, "dp", axis=0, tiled=True),
        lax.all_gather(bias_out, "dp", axis=0, tiled=True),
        lax.all_gather(w_up, "dp", axis=0, tiled=True),
        lax.all_gather(bias_up, "dp", axis=0, tiled=True),
        lax.all_gather(w_down, "dp", axis=0, tiled=True),
        lax.all_gather(bias_down, "dp", axis=0, tiled=True),
        lax.all_gather(gain_attn, "dp", axis=0, tiled=True),
        lax.all_gather(shift_attn, "dp", axis=0, tiled=True),
        lax.all_gather(gain_ffn, "dp", axis=0, tiled=True),
        lax.all_gather(shift_ffn, "dp", axis=0, tiled=True),
    )
    gain_first = full_gain_one.astype(jnp.float32)
    shift_first = full_shift_one.astype(jnp.float32)
    gain_second = full_gain_two.astype(jnp.float32)
    shift_second = full_shift_two.astype(jnp.float32)
    projected = matmul(inputs, full_qkv).reshape(rows_dev, 3, width)
    bias_rows = full_bqv.astype(jnp.float32)
    added = jnp.stack([bias_rows[:width], jnp.zeros((width,), jnp.float32), bias_rows[width:]])
    qkv_low = (
        (projected + added[None]).astype(jnp.bfloat16).reshape(rows_dev, 3, groups, head_width)
    )
    regrouped = lax.all_to_all(qkv_low, "seq", split_axis=2, concat_axis=0, tiled=True)
    queries = regrouped[:, 0, 0].reshape(slot_rows, heads_dev, HD)
    keys_all = regrouped[:, 1, 0].reshape(slot_rows, heads_dev, HD)
    values_all = regrouped[:, 2, 0].reshape(slot_rows, heads_dev, HD)
    positions = jnp.arange(slot_rows)
    key_bias = jnp.where(positions < lengths[0], 0.0, -1000000000.0).astype(jnp.float32)
    block_rows = min(512, slot_rows)
    block_count = slot_rows // block_rows
    query_blocks = queries.reshape(block_count, block_rows, heads_dev, HD)

    def score_block(query_block):
        scores = jnp.einsum(
            "qhe,khe->hqk", query_block, keys_all, preferred_element_type=jnp.float32
        )
        return scores * scale + key_bias

    def attend(query_block):
        scores = score_block(query_block)
        largest = jnp.max(scores, axis=-1, keepdims=True)
        exponent = jnp.exp(scores - largest)
        totals = jnp.sum(exponent, axis=-1, keepdims=True)
        weights_soft = exponent / totals
        context = jnp.einsum(
            "hqk,khe->qhe",
            weights_soft.astype(jnp.bfloat16),
            values_all,
            preferred_element_type=jnp.float32,
        )
        return (context.astype(jnp.bfloat16), largest + jnp.log(totals))

    contexts, log_totals = lax.map(attend, query_blocks)
    context_low = contexts.reshape(slot_rows, 1, head_width)
    returned = lax.all_to_all(context_low, "seq", split_axis=0, concat_axis=1, tiled=True).reshape(
        rows_dev, width
    )
    attn_branch = matmul(returned, full_wout) + full_bout.astype(jnp.float32)
    resid_one = inputs.astype(jnp.float32) + attn_branch
    hidden_one, first_pull = jax.vjp(layer_norm, resid_one, gain_first, shift_first)
    hidden_low = hidden_one.astype(jnp.bfloat16)
    pre_act = matmul(hidden_low, full_wup) + full_bup.astype(jnp.float32)
    activated, gelu_pull = jax.vjp(gelu_exact, pre_act)
    act_low = activated.astype(jnp.bfloat16)
    ffn_branch = matmul(act_low, full_wdown) + full_bdown.astype(jnp.float32)
    resid_two = hidden_one + ffn_branch
    output, second_pull = jax.vjp(layer_norm, resid_two, gain_second, shift_second)
    grad_two, grad_gain_two, grad_shift_two = second_pull(cotangent[0].astype(jnp.float32))
    grad_branch = grad_two.astype(jnp.bfloat16)
    grad_wdown = matmul_tn(act_low, grad_branch)
    grad_bdown = column_sum(grad_branch)
    (grad_pre,) = gelu_pull(matmul_nt(grad_branch, full_wdown))
    grad_pre_low = grad_pre.astype(jnp.bfloat16)
    grad_wup = matmul_tn(hidden_low, grad_pre_low)
    grad_bup = column_sum(grad_pre_low)
    grad_hidden = grad_two + matmul_nt(grad_pre_low, full_wup)
    grad_one, grad_gain_one, grad_shift_one = first_pull(grad_hidden)
    grad_proj = grad_one.astype(jnp.bfloat16)
    grad_wout = matmul_tn(returned, grad_proj)
    grad_bout = column_sum(grad_proj)
    grad_context = (
        matmul_nt(grad_proj, full_wout).astype(jnp.bfloat16).reshape(rows_dev, groups, head_width)
    )
    grad_heads = lax.all_to_all(grad_context, "seq", split_axis=1, concat_axis=0, tiled=True)
    grad_blocks = grad_heads.reshape(block_count, block_rows, heads_dev, HD)

    def attend_back(carry, item):
        grad_keys, grad_values = carry
        query_block, grad_block, log_block = item
        weights_soft = jnp.exp(score_block(query_block) - log_block)
        soft_low = weights_soft.astype(jnp.bfloat16)
        grad_values = grad_values + jnp.einsum(
            "hqk,qhe->khe", soft_low, grad_block, preferred_element_type=jnp.float32
        )
        grad_soft = jnp.einsum(
            "qhe,khe->hqk", grad_block, values_all, preferred_element_type=jnp.float32
        )
        inner = jnp.sum(weights_soft * grad_soft, axis=-1, keepdims=True)
        grad_scores = (weights_soft * (grad_soft - inner)).astype(jnp.bfloat16)
        grad_query = (
            jnp.einsum("hqk,khe->qhe", grad_scores, keys_all, preferred_element_type=jnp.float32)
            * scale
        )
        grad_keys = (
            grad_keys
            + jnp.einsum(
                "hqk,qhe->khe", grad_scores, query_block, preferred_element_type=jnp.float32
            )
            * scale
        )
        return ((grad_keys, grad_values), grad_query)

    zeros_grad = jnp.zeros((slot_rows, heads_dev, HD), jnp.float32)
    (grad_keys, grad_values), grad_queries = lax.scan(
        attend_back, (zeros_grad, zeros_grad), (query_blocks, grad_blocks, log_totals)
    )
    grad_stack = jnp.stack(
        [
            grad_queries.reshape(slot_rows, head_width),
            grad_keys.reshape(slot_rows, head_width),
            grad_values.reshape(slot_rows, head_width),
        ],
        axis=1,
    )
    grad_stack = grad_stack.astype(jnp.bfloat16).reshape(slot_rows, 3, 1, head_width)
    grad_qkv = lax.all_to_all(grad_stack, "seq", split_axis=0, concat_axis=2, tiled=True).reshape(
        rows_dev, 3 * width
    )
    grad_wqkv = matmul_tn(inputs, grad_qkv)
    summed_qkv = column_sum(grad_qkv)
    grad_bqv = jnp.concatenate([summed_qkv[:width], summed_qkv[2 * width :]])
    grad_inputs = grad_one + matmul_nt(grad_qkv, full_qkv)
    shares = (
        lax.psum_scatter(grad_wqkv, "dp", scatter_dimension=0, tiled=True),
        lax.psum_scatter(grad_bqv, "dp", scatter_dimension=0, tiled=True),
        lax.psum_scatter(grad_wout, "dp", scatter_dimension=0, tiled=True),
        lax.psum_scatter(grad_bout, "dp", scatter_dimension=0, tiled=True),
        lax.psum_scatter(grad_wup, "dp", scatter_dimension=0, tiled=True),
        lax.psum_scatter(grad_bup, "dp", scatter_dimension=0, tiled=True),
        lax.psum_scatter(grad_wdown, "dp", scatter_dimension=0, tiled=True),
        lax.psum_scatter(grad_bdown, "dp", scatter_dimension=0, tiled=True),
        lax.psum_scatter(grad_gain_one, "dp", scatter_dimension=0, tiled=True),
        lax.psum_scatter(grad_shift_one, "dp", scatter_dimension=0, tiled=True),
        lax.psum_scatter(grad_gain_two, "dp", scatter_dimension=0, tiled=True),
        lax.psum_scatter(grad_shift_two, "dp", scatter_dimension=0, tiled=True),
    )
    (
        share_qkv,
        share_bqv,
        share_wout,
        share_bout,
        share_wup,
        share_bup,
        share_wdown,
        share_bdown,
        share_gain_one,
        share_shift_one,
        share_gain_two,
        share_shift_two,
    ) = shares
    shards = (
        lax.psum(share_qkv.astype(jnp.bfloat16), "seq").astype(jnp.float32),
        lax.psum(share_bqv.astype(jnp.bfloat16), "seq").astype(jnp.float32),
        lax.psum(share_wout.astype(jnp.bfloat16), "seq").astype(jnp.float32),
        lax.psum(share_bout.astype(jnp.bfloat16), "seq").astype(jnp.float32),
        lax.psum(share_wup.astype(jnp.bfloat16), "seq").astype(jnp.float32),
        lax.psum(share_bup.astype(jnp.bfloat16), "seq").astype(jnp.float32),
        lax.psum(share_wdown.astype(jnp.bfloat16), "seq").astype(jnp.float32),
        lax.psum(share_bdown.astype(jnp.bfloat16), "seq").astype(jnp.float32),
        lax.psum(share_gain_one.astype(jnp.bfloat16), "seq").astype(jnp.float32),
        lax.psum(share_shift_one.astype(jnp.bfloat16), "seq").astype(jnp.float32),
        lax.psum(share_gain_two.astype(jnp.bfloat16), "seq").astype(jnp.float32),
        lax.psum(share_shift_two.astype(jnp.bfloat16), "seq").astype(jnp.float32),
    )
    return (output.astype(jnp.bfloat16)[None], grad_inputs[None]) + tuple(shards)


def solution(mesh):
    in_specs = (
        P("dp", "seq", None),
        P("dp"),
        P("dp", None),
        P("dp"),
        P("dp", None),
        P("dp"),
        P("dp", None),
        P("dp"),
        P("dp", None),
        P("dp"),
        P("dp"),
        P("dp"),
        P("dp"),
        P("dp"),
        P("dp", "seq", None),
    )
    out_specs = (
        P("dp", "seq", None),
        P("dp", "seq", None),
        P("dp", None),
        P("dp"),
        P("dp", None),
        P("dp"),
        P("dp", None),
        P("dp"),
        P("dp", None),
        P("dp"),
        P("dp"),
        P("dp"),
        P("dp"),
        P("dp"),
    )
    return jax.shard_map(local, mesh=mesh, in_specs=in_specs, out_specs=out_specs, check_vma=False)
```

profile of v0, /device:TPU:0, one launch (start us, length us, event | category | flops | bytes accessed | tf_op | source)
XLA Modules:
  0.0 1252.8 jit_solution(12332146206228527504)
XLA Ops:
  19.4 63.7 %all-reduce.17 = (bf16[1536]{0:T(1024)(128)(2,1)S(1)}, bf16[768]{0:T(1024)(128)(2,1)}, bf16[768]{0:T(1024)(128)(2,1)}, bf16[768]{0:T(1024)(128)(2,1)}, bf16[3072...) all-reduce(bf16[1536]{0:T(1024)(128)(2,1)S(1)} %dynamic-update-slic, ...), channel_id=1, replica_groups=mesh['seq'=2,'dp'=16] {'dp'}, use_global_device_ids=true, to_apply=%add | all-reduce | flops 9216 | bytes 36864
  107.7 48.3 %all-to-all-done = bf16[1024,3,2,384]{3,0,1,2:T(8,128)(2,1)} async-done(((bf16[1024,3,2,384]{3,0,1,2:T(8,128)(2,1)}), bf16[1024,3,2,384]{3,0,1,2:T(8,128)(2,1)}, u32[]{:S(2)}, u32[]{:S(2)}) %all-to-all-start) | async-done | bytes 4718624 | tf_op jit(solution)/shard_map/all_to_all | solution.py:104
  173.3 106.9 %while.28 = (s32[]{:T(128)}, bf16[4,512,6,64]{1,3,2,0:T(8,128)(2,1)}, f32[4,6,512,1]{2,1,3,0:T(8,128)S(1)}, bf16[4,512,6,64]{1,3,2,0:T(8,128)(2,1)}, bf16[2048,6...) while((s32[]{:T(128)}, bf16[4,512,6,64]{1,3,2,0:T(8,128)(2,1)}, ...), condition=%wide.region_3.4_spmd.clone, body=%wide.region_0.3_spmd.clone.sunk | while | flops 1686307840 | bytes 180237424 | solution.py:134
  188.1 12.5 fusion.115
  320.9 13.6 %multiply_convert_fusion.1 = (bf16[1024,3072]{1,0:T(8,128)(2,1)}, f32[1024,3072]{1,0:T(8,128)}) fusion(f32[3072]{0:T(1024)S(1)} %convert_element_type.172, bf16[768,3072]{1,0:T(8,128)(2,1)} %all-gather.9.cloned.1.call-done, f32[1024,768]{0,1:T(8,128)} %copy-done.9, f32[768]{0:T(1024)S(1)} %convert_element_type.170, f32[768]{0:T(1024)S(1)} %convert_element_type.169, ...), kind=kOutput, calls=%fused_computation.49 | convolution fusion | flops 4854644736 | bytes 26765312 | tf_op jit(solution)/shard_map/dot_general | solution.py:23
  350.3 15.8 %convert_reduce_fusion = (f32[3072]{0:T(1024)}, bf16[1024,3072]{1,0:T(8,128)(2,1)S(1)}) fusion(bf16[1024,768]{0,1:T(8,128)(2,1)S(1)} %get-tuple-element.403, bf16[3072,768]{1,0:T(8,128)(2,1)S(1)} %bitcast.200, f32[1024,3072]{1,0:T(8,128)} %get-tuple-element.427, f32[3072]{0:T(1024)S(1)} %convert_element_type.172), kind=kOutput, calls=%fused_computation.47 | convolution fusion | flops 4882166784 | bytes 25190400 | tf_op jit(solution)/shard_map/dot_general | solution.py:33
  407.1 328.5 %while.29 = (s32[]{:T(128)}, f32[2048,6,64]{0,2,1:T(8,128)}, f32[2048,6,64]{0,2,1:T(8,128)}, bf16[4,512,6,64]{1,3,2,0:T(8,128)(2,1)}, bf16[4,512,6,64]{1,3,2,0:T...) while((s32[]{:T(128)}, f32[2048,6,64]{0,2,1:T(8,128)}, ...), condition=%wide.region_14.15_spmd.clone, body=%wide.region_12.14_spmd.clone.sunk | while | flops 4125033472 | bytes 208525968 | solution.py:195
  419.1 17.0 %multiply_reduce_fusion.6 = (f32[6,512]{1,0:T(8,128)S(1)}, f32[6,512,2048]{2,1,0:T(8,128)}) fusion(f32[6,512,2048]{2,1,0:T(8,128)} %fusion.125, f32[6,512]{1,0:T(8,128)S(1)} %dynamic-slice_bitcast_fusion.2, f32[2048]{0:T(1024)S(1)} %fusion.126, bf16[2048,6,64]{0,2,1:T(8,128)(2,1)S(1)} %get-tuple-element.601, ...), kind=kOutput, calls=%fused_computation.20.clone.1 | convolution fusion | flops 836760576 | bytes 52331008 | tf_op jit(solution)/shard_map/while/body/eval_jaxpr/qhe,khe->hqk/dot_general | solution.py:176
  436.1 21.6 %multiply_convert_fusion.3 = bf16[6,512,2048]{2,1,0:T(8,128)(2,1)} fusion(f32[6,512,2048]{2,1,0:T(8,128)} %get-tuple-element.543, f32[6,512,2048]{2,1,0:T(8,128)} %fusion.125, f32[6,512]{1,0:T(8,128)S(1)} %get-tuple-element.544, f32[6,512]{1,0:T(8,128)S(1)} %dynamic-slice_bitcast_fusion.2, f32[2048]{0:T(1024)S(1)} %fusion.126), kind=kLoop, calls=%fused_computation.19.clone.1 | loop fusion | flops 37748736 | bytes 62947328 | tf_op jit(solution)/shard_map/while/body/eval_jaxpr/convert_element_type | solution.py:180
  475.7 12.4 bitcast_add_fusion.5
  499.9 16.6 %multiply_reduce_fusion.6 = (f32[6,512]{1,0:T(8,128)S(1)}, f32[6,512,2048]{2,1,0:T(8,128)}) fusion(f32[6,512,2048]{2,1,0:T(8,128)} %fusion.125, f32[6,512]{1,0:T(8,128)S(1)} %dynamic-slice_bitcast_fusion.2, f32[2048]{0:T(1024)S(1)} %fusion.126, bf16[2048,6,64]{0,2,1:T(8,128)(2,1)S(1)} %get-tuple-element.601, ...), kind=kOutput, calls=%fused_computation.20.clone.1 | convolution fusion | flops 836760576 | bytes 52331008 | tf_op jit(solution)/shard_map/while/body/eval_jaxpr/qhe,khe->hqk/dot_general | solution.py:176
  516.5 21.3 %multiply_convert_fusion.3 = bf16[6,512,2048]{2,1,0:T(8,128)(2,1)} fusion(f32[6,512,2048]{2,1,0:T(8,128)} %get-tuple-element.543, f32[6,512,2048]{2,1,0:T(8,128)} %fusion.125, f32[6,512]{1,0:T(8,128)S(1)} %get-tuple-element.544, f32[6,512]{1,0:T(8,128)S(1)} %dynamic-slice_bitcast_fusion.2, f32[2048]{0:T(1024)S(1)} %fusion.126), kind=kLoop, calls=%fused_computation.19.clone.1 | loop fusion | flops 37748736 | bytes 62947328 | tf_op jit(solution)/shard_map/while/body/eval_jaxpr/convert_element_type | solution.py:180
  556.7 13.8 %bitcast_add_fusion.5 = f32[2048,6,64]{0,2,1:T(8,128)} fusion(f32[2048,6,64]{0,2,1:T(8,128)} %get-tuple-element.583, f32[6,512,2048]{2,1,0:T(8,128)} %fusion.125, f32[6,512]{1,0:T(8,128)S(1)} %dynamic-slice_bitcast_fusion.2, f32[2048]{0:T(1024)S(1)} %fusion.126, pred[]{:T(512)S(6)} %compare.3, bf16[4,512,6,64]{1,3,2,0:T(8,128)(2,1)} %get-tuple-element.600, ...), kind=kOutput, calls=%fused_computation.24.clone.1 | convolution fusion | flops 832045056 | bytes 31871488 | tf_op jit(solution)/shard_map/while/body/eval_jaxpr/hqk,qhe->khe/dot_general | solution.py:173
  582.4 16.6 %multiply_reduce_fusion.6 = (f32[6,512]{1,0:T(8,128)S(1)}, f32[6,512,2048]{2,1,0:T(8,128)}) fusion(f32[6,512,2048]{2,1,0:T(8,128)} %fusion.125, f32[6,512]{1,0:T(8,128)S(1)} %dynamic-slice_bitcast_fusion.2, f32[2048]{0:T(1024)S(1)} %fusion.126, bf16[2048,6,64]{0,2,1:T(8,128)(2,1)S(1)} %get-tuple-element.601, ...), kind=kOutput, calls=%fused_computation.20.clone.1 | convolution fusion | flops 836760576 | bytes 52331008 | tf_op jit(solution)/shard_map/while/body/eval_jaxpr/qhe,khe->hqk/dot_general | solution.py:176
  599.0 21.3 %multiply_convert_fusion.3 = bf16[6,512,2048]{2,1,0:T(8,128)(2,1)} fusion(f32[6,512,2048]{2,1,0:T(8,128)} %get-tuple-element.543, f32[6,512,2048]{2,1,0:T(8,128)} %fusion.125, f32[6,512]{1,0:T(8,128)S(1)} %get-tuple-element.544, f32[6,512]{1,0:T(8,128)S(1)} %dynamic-slice_bitcast_fusion.2, f32[2048]{0:T(1024)S(1)} %fusion.126), kind=kLoop, calls=%fused_computation.19.clone.1 | loop fusion | flops 37748736 | bytes 62947328 | tf_op jit(solution)/shard_map/while/body/eval_jaxpr/convert_element_type | solution.py:180
  639.2 13.7 %bitcast_add_fusion.5 = f32[2048,6,64]{0,2,1:T(8,128)} fusion(f32[2048,6,64]{0,2,1:T(8,128)} %get-tuple-element.583, f32[6,512,2048]{2,1,0:T(8,128)} %fusion.125, f32[6,512]{1,0:T(8,128)S(1)} %dynamic-slice_bitcast_fusion.2, f32[2048]{0:T(1024)S(1)} %fusion.126, pred[]{:T(512)S(6)} %compare.3, bf16[4,512,6,64]{1,3,2,0:T(8,128)(2,1)} %get-tuple-element.600, ...), kind=kOutput, calls=%fused_computation.24.clone.1 | convolution fusion | flops 832045056 | bytes 31871488 | tf_op jit(solution)/shard_map/while/body/eval_jaxpr/hqk,qhe->khe/dot_general | solution.py:173
  664.8 16.6 %multiply_reduce_fusion.6 = (f32[6,512]{1,0:T(8,128)S(1)}, f32[6,512,2048]{2,1,0:T(8,128)}) fusion(f32[6,512,2048]{2,1,0:T(8,128)} %fusion.125, f32[6,512]{1,0:T(8,128)S(1)} %dynamic-slice_bitcast_fusion.2, f32[2048]{0:T(1024)S(1)} %fusion.126, bf16[2048,6,64]{0,2,1:T(8,128)(2,1)S(1)} %get-tuple-element.601, ...), kind=kOutput, calls=%fused_computation.20.clone.1 | convolution fusion | flops 836760576 | bytes 52331008 | tf_op jit(solution)/shard_map/while/body/eval_jaxpr/qhe,khe->hqk/dot_general | solution.py:176
  681.4 21.3 %multiply_convert_fusion.3 = bf16[6,512,2048]{2,1,0:T(8,128)(2,1)} fusion(f32[6,512,2048]{2,1,0:T(8,128)} %get-tuple-element.543, f32[6,512,2048]{2,1,0:T(8,128)} %fusion.125, f32[6,512]{1,0:T(8,128)S(1)} %get-tuple-element.544, f32[6,512]{1,0:T(8,128)S(1)} %dynamic-slice_bitcast_fusion.2, f32[2048]{0:T(1024)S(1)} %fusion.126), kind=kLoop, calls=%fused_computation.19.clone.1 | loop fusion | flops 37748736 | bytes 62947328 | tf_op jit(solution)/shard_map/while/body/eval_jaxpr/convert_element_type | solution.py:180
  721.6 13.8 %bitcast_add_fusion.5 = f32[2048,6,64]{0,2,1:T(8,128)} fusion(f32[2048,6,64]{0,2,1:T(8,128)} %get-tuple-element.583, f32[6,512,2048]{2,1,0:T(8,128)} %fusion.125, f32[6,512]{1,0:T(8,128)S(1)} %dynamic-slice_bitcast_fusion.2, f32[2048]{0:T(1024)S(1)} %fusion.126, pred[]{:T(512)S(6)} %compare.3, bf16[4,512,6,64]{1,3,2,0:T(8,128)(2,1)} %get-tuple-element.600, ...), kind=kOutput, calls=%fused_computation.24.clone.1 | convolution fusion | flops 832045056 | bytes 31871488 | tf_op jit(solution)/shard_map/while/body/eval_jaxpr/hqk,qhe->khe/dot_general | solution.py:173
  758.6 67.7 %all_to_all.63 = bf16[2048,3,1,384]{3,1,2,0:T(4,128)(2,1)S(1)} all-to-all(bf16[2048,3,1,384]{3,1,2,0:T(4,128)(2,1)} %copy.150), channel_id=1, replica_groups=mesh['seq'=2,'dp'=16] {'seq'}, dimensions={0} | all-to-all | bytes 9437184 | tf_op jit(solution)/shard_map/all_to_all | solution.py:207
  883.9 78.7 %all-reduce.16 = (bf16[1536]{0:T(1024)(128)(2,1)S(1)}, bf16[768]{0:T(1024)(128)(2,1)S(1)}, bf16[3072]{0:T(1024)(128)(2,1)S(1)}, bf16[768]{0:T(1024)(128)(2,1)S(1...) all-reduce(f32[1536]{0:T(1024)S(1)} %pad_maximum_fusion.2, ...), channel_id=3, replica_groups=mesh['seq'=2,'dp'=16] {'dp'}, use_global_device_ids=true, to_apply=%region_18.19.clone | all-reduce | flops 9216 | bytes 55296
  976.3 98.3 %reduce-scatter.9.cloned.1.call-done = f32[48,3072]{1,0:T(8,128)} async-done(((f32[768,3072]{1,0:T(8,128)}), f32[48,3072]{1,0:T(8,128)}) %reduce-scatter.9.cloned.1.call-update) | async-done | bytes 589840 | tf_op jit(solution)/shard_map/reduce_scatter | solution.py:219
  1076.3 114.0 %reduce-scatter.11.cloned.1.call-done = f32[192,768]{1,0:T(8,128)} async-done(((f32[3072,768]{1,0:T(8,128)}), f32[192,768]{1,0:T(8,128)}) %reduce-scatter.11.cloned.1.call-update) | async-done | bytes 589840 | tf_op jit(solution)/shard_map/reduce_scatter | solution.py:221
  1204.6 34.2 %all-reduce.22.cloned.1.call-done = (bf16[48,2304]{0,1:T(8,128)(2,1)}, bf16[48,768]{1,0:T(8,128)(2,1)}, bf16[48,3072]{1,0:T(8,128)(2,1)}, bf16[192,768]{1,0:T(8,128)(2,1)}) async-done(((bf16[48,2304]{0,1:T(8,128)(2,1)}, bf16[48,768]{1,0:T(8,128)(2,1)}, bf16[48,3072]{1,0:T(8,128)(2,1)}, bf16[192,768]{1,0:T(8,128)(2,1)}), (bf16[48,2304]{0,1:T(8,128)(2,1)}, bf16[48,768]{1,0:T(8,128)(2,1)}, ...) | async-done | bytes 884752 | tf_op jit(solution)/shard_map/psum | solution.py:243
  (296 shorter events, 480.3 us)
Async XLA Ops:
  7.2 76.1 %all-gather.5.cloned.1.call-start = ((), (), s32[]{:S(2)}) async-start(), calls=%async_computation.8 | async-start | bytes 3760128 | tf_op jit(solution)/shard_map/all_gather | solution.py:81
  7.9 307.0 %all-gather.7.cloned.1.call-start = ((), (), s32[]{:S(2)}) async-start(), calls=%async_computation.9 | async-start | bytes 1253376 | tf_op jit(solution)/shard_map/all_gather | solution.py:83
  8.7 312.2 %all-gather.9.cloned.1.call-start = ((), (), s32[]{:S(2)}) async-start(), calls=%async_computation.10 | async-start | bytes 5013504 | tf_op jit(solution)/shard_map/all_gather | solution.py:85
  101.3 54.7 %all-to-all-start = ((bf16[1024,3,2,384]{3,0,1,2:T(8,128)(2,1)}), bf16[1024,3,2,384]{3,0,1,2:T(8,128)(2,1)}, u32[]{:S(2)}, u32[]{:S(2)}) async-start(bf16[1024,3,2,384]{3,0,1,2:T(8,128)(2,1)} %copy.135), calls=%async_computation | async-start | bytes 9437184 | tf_op jit(solution)/shard_map/all_to_all | solution.py:104
  107.1 227.4 %all-gather.11.cloned.1.call-start = ((), (), s32[]{:S(2)}) async-start(), calls=%async_computation.11 | async-start | bytes 5013504 | tf_op jit(solution)/shard_map/all_gather | solution.py:87
  179.1 8.9 copy-start
  290.4 18.3 %all-to-all-start.1 = ((bf16[2,2,196608]{2,1,0:T(2,128)(2,1)}), bf16[2,2,196608]{2,1,0:T(2,128)(2,1)S(1)}, u32[]{:S(2)}, u32[]{:S(2)}) async-start(bf16[2,2,196608]{2,1,0:T(2,128)(2,1)} %reshape.258), calls=%async_computation.1 | async-start | bytes 3145728 | tf_op jit(solution)/shard_map/all_to_all | solution.py:136
  296.0 77.3 %copy-start.24 = (f32[768]{0:T(1024)}, f32[768]{0:T(1024)S(1)}, u32[]{:S(2)}) copy-start(f32[768]{0:T(1024)S(1)} %convert_element_type.169) | copy-start | bytes 9220
  296.1 38.4 %copy-start.33 = (f32[768]{0:T(1024)}, f32[768]{0:T(1024)S(1)}, u32[]{:S(2)}) copy-start(f32[768]{0:T(1024)S(1)} %convert_element_type.170) | copy-start | bytes 9220
  297.9 68.2 %copy-start.5 = (bf16[1,1024,768]{1,2,0:T(8,128)(2,1)}, bf16[1,1024,768]{1,2,0:T(8,128)(2,1)S(1)}, u32[]{:S(2)}) copy-start(bf16[1,1024,768]{1,2,0:T(8,128)(2,1)S(1)} %copy.144) | copy-start | bytes 4718596
  318.8 54.5 %copy-start.20 = (f32[1024]{0:T(1024)}, f32[1024]{0:T(1024)S(1)}, u32[]{:S(2)}) copy-start(f32[1024]{0:T(1024)S(1)} %broadcast_multiply_fusion.1) | copy-start | bytes 12292
  320.9 52.5 %copy-start.26 = (f32[1024]{0:T(1024)}, f32[1024]{0:T(1024)S(1)}, u32[]{:S(2)}) copy-start(f32[1024]{0:T(1024)S(1)} %fusion.49) | copy-start | bytes 12292
  347.0 19.1 %slice-start = ((s8[4718592]{0:T(1024)(128)(4,1)}), s8[4194304]{0:T(1024)(128)(4,1)S(1)}, s32[]{:S(2)}) async-start(s8[4718592]{0:T(1024)(128)(4,1)} %bitcast.197), calls=%async_computation.17 | async-start | bytes 8388608
  350.3 15.8 %copy-start.17 = (bf16[1024,768]{0,1:T(8,128)(2,1)}, bf16[1024,768]{0,1:T(8,128)(2,1)S(1)}, u32[]{:S(2)}) copy-start(bf16[1024,768]{0,1:T(8,128)(2,1)S(1)} %get-tuple-element.403) | copy-start | bytes 4718596
  350.3 15.8 %copy-start.10 = (f32[1024,768]{0,1:T(8,128)S(1)}, f32[1024,768]{0,1:T(8,128)}, u32[]{:S(2)}) copy-start(f32[1024,768]{0,1:T(8,128)} %copy-done.9) | copy-start | bytes 9437188
  350.3 15.8 %slice-start.1 = ((s8[4718592]{0:T(1024)(128)(4,1)}), s8[524288]{0:T(1024)(128)(4,1)S(1)}, s32[]{:S(2)}) async-start(s8[4718592]{0:T(1024)(128)(4,1)} %bitcast.197), calls=%async_computation.18 | async-start | bytes 1048576
  378.8 17.2 %all-to-all-start.2 = ((bf16[1024,2,384]{0,2,1:T(8,128)(2,1)}), bf16[1024,2,384]{0,2,1:T(8,128)(2,1)S(1)}, u32[]{:S(2)}, u32[]{:S(2)}) async-start(bf16[1024,2,384]{0,2,1:T(8,128)(2,1)} %bitcast.196), calls=%async_computation.2 | async-start | bytes 3145728 | tf_op jit(solution)/shard_map/all_to_all | solution.py:165
  382.7 589.9 %reduce-scatter.7.cloned.1.call-start = ((), (), s32[]{:S(2)}) async-start(), calls=%async_computation.12 | async-start | bytes 2506752 | tf_op jit(solution)/shard_map/reduce_scatter | solution.py:217
  387.0 587.1 %reduce-scatter.13.cloned.1.call-start = ((), (), s32[]{:S(2)}) async-start(), calls=%async_computation.15 | async-start | bytes 7520256
  851.9 222.6 %reduce-scatter.9.cloned.1.call-start = ((), (), s32[]{:S(2)}) async-start(), calls=%async_computation.13 | async-start | bytes 10027008 | tf_op jit(solution)/shard_map/reduce_scatter | solution.py:219
  864.4 325.9 %reduce-scatter.11.cloned.1.call-start = ((), (), s32[]{:S(2)}) async-start(), calls=%async_computation.14 | async-start | bytes 10027008 | tf_op jit(solution)/shard_map/reduce_scatter | solution.py:221
  876.0 362.8 %all-reduce.22.cloned.1.call-start = ((), (), s32[]{:S(2)}) async-start(), calls=%async_computation.16 | async-start | bytes 2506752 | tf_op jit(solution)/shard_map/psum | solution.py:243
  883.8 308.3 %copy-start.8 = (f32[1024,768]{0,1:T(8,128)S(1)}, f32[1024,768]{0,1:T(8,128)}, u32[]{:S(2)}) copy-start(f32[1024,768]{0,1:T(8,128)} %copy-done.7) | copy-start | bytes 9437188
  883.8 308.3 %copy-start.23 = (f32[1024]{0:T(1024)S(1)}, f32[1024]{0:T(1024)}, u32[]{:S(2)}) copy-start(f32[1024]{0:T(1024)} %copy-done.22) | copy-start | bytes 12292
  (40 other events, 179.8 us)
Sparse Core Ops, SparseCore 0:
  10.3 50.6 all-gather.4
  63.2 36.8 all-gather.6
  102.4 52.3 all-gather.8
  156.9 51.9 all-gather.10
  387.2 68.0 reduce-scatter.6
  852.1 106.9 reduce-scatter.12
  963.2 111.2 reduce-scatter.8
  1079.2 111.1 reduce-scatter.10
  1194.0 44.7 all-reduce.21
where the time goes:
time: 1260 us; the launch traced here: 1250 us
  matrix products  411 us (33%)
  waiting for transfers between devices  317 us (25%)
  blocking collectives  215 us (17%)
  other arithmetic  145 us (12%)
  local copies, waits for them, and re-layouts  130 us (10%)
  between operations  19.3 us (2%)
  starting transfers between devices  14.5 us (1%)
    unnamed x2, blocking collectives  142 us
    reduce_scatter x1, waiting for transfers between devices, local(): lax.psum_scatter(grad_wdown, 'dp', scatter_dimension=0, tiled=True)  114 us
    reduce_scatter x1, waiting for transfers between devices, local(): lax.psum_scatter(grad_wup, 'dp', scatter_dimension=0, tiled=True)  98.3 us
    convert_element_type x4, other arithmetic, attend_back(): grad_scores = (weights_soft * (grad_soft - inner)).astype(jnp.bfloat16)  85.6 us
    all_to_all x1, blocking collectives, local(): lax.all_to_all(grad_stack, 'seq', split_axis=0, concat_axis=2, tiled=True)  67.7 us
    dot_general x4, matrix products, attend_back(): jnp.einsum('qhe,khe->hqk', grad_block, values_all, preferred_element_type...  66.7 us
    dot_general x8, matrix products, score_block(): jnp.einsum('qhe,khe->hqk', query_block, keys_all, preferred_element_type=...  65.5 us
    dot_general x4, matrix products, attend_back(): jnp.einsum('hqk,qhe->khe', soft_low, grad_block, preferred_element_type=j...  53.7 us
  transfers between devices with their start and end apart: 12, of which 6 were waited for; matrix products, arithmetic and copies ran while one was open for 49% of the time, Pallas kernels for 0%

commit v1 on v0

--- a/solution.py
+++ b/solution.py
@@ -240,7 +240,7 @@
         share_shift_two,
     ) = shares
     shards = (
-        lax.psum(share_qkv.astype(jnp.bfloat16), "seq").astype(jnp.float32),
+        jnp.sum(lax.all_gather(share_qkv.astype(jnp.bfloat16), "seq"), axis=0).astype(jnp.float32),
         lax.psum(share_bqv.astype(jnp.bfloat16), "seq").astype(jnp.float32),
         lax.psum(share_wout.astype(jnp.bfloat16), "seq").astype(jnp.float32),
         lax.psum(share_bout.astype(jnp.bfloat16), "seq").astype(jnp.float32),

time: 1260 us -> 1040 us (0.83)
  waiting for transfers between devices: 317 us -> 79.8 us
    reduce_scatter x1, waiting for transfers between devices: 114 us -> 0.02 us  [local(): lax.psum_scatter(grad_wdown, 'dp', scatter_dimension=0, tiled=True)]
    reduce_scatter x1, waiting for transfers between devices: 98.3 us -> 0.01 us  [local(): lax.psum_scatter(grad_wup, 'dp', scatter_dimension=0, tiled=True)]
    psum x1, waiting for transfers between devices: 34.2 us -> 16.4 us  [local(): lax.psum(share_wout.astype(jnp.bfloat16), 'seq').astype(jnp.float32)]
    unnamed x134 -> x118, local copies, waits for them, and re-layouts: 51.3 us -> 47.2 us
  transfers between devices with their start and end apart: 12 -> 12, of which waited for: 6 -> 4; matrix products, arithmetic and copies ran while one was open for 49% -> 61% of each run, Pallas kernels for 0% -> 0%
where the time goes in v1:
time: 1040 us
  matrix products  415 us (40%)
  blocking collectives  226 us (22%)
  other arithmetic  155 us (15%)
  local copies, waits for them, and re-layouts  129 us (12%)
  waiting for transfers between devices  79.8 us (8%)
  between operations  18.7 us (2%)
  starting transfers between devices  14.4 us (1%)
    unnamed x2, blocking collectives  143 us
    convert_element_type x4, other arithmetic, attend_back(): grad_scores = (weights_soft * (grad_soft - inner)).astype(jnp.bfloat16)  91 us
    dot_general x4, matrix products, attend_back(): jnp.einsum('qhe,khe->hqk', grad_block, values_all, preferred_element_type...  67.6 us
    all_to_all x1, blocking collectives, local(): lax.all_to_all(grad_stack, 'seq', split_axis=0, concat_axis=2, tiled=True)  67 us
    dot_general x8, matrix products, score_block(): jnp.einsum('qhe,khe->hqk', query_block, keys_all, preferred_element_type=...  65.8 us
    dot_general x4, matrix products, attend_back(): jnp.einsum('hqk,qhe->khe', soft_low, grad_block, preferred_element_type=j...  55.9 us
    dot_general x4, matrix products, attend(): jnp.einsum('hqk,khe->qhe', weights_soft.astype(jnp.bfloat16), values_all,...  49.5 us
    all_to_all x1, waiting for transfers between devices, local(): lax.all_to_all(qkv_low, 'seq', split_axis=2, concat_axis=0, tiled=True)  48.3 us
  transfers between devices with their start and end apart: 12, of which 4 were waited for; matrix products, arithmetic and copies ran while one was open for 61% of the time, Pallas kernels for 0%

profile of v1, /device:TPU:0, one launch (start us, length us, event | category | flops | bytes accessed | tf_op | source)
XLA Modules:
  0.0 1037.9 jit_solution(17010687925323031058)
XLA Ops:
  19.4 63.7 %all-reduce.17 = (bf16[1536]{0:T(1024)(128)(2,1)S(1)}, bf16[768]{0:T(1024)(128)(2,1)}, bf16[768]{0:T(1024)(128)(2,1)}, bf16[768]{0:T(1024)(128)(2,1)}, bf16[3072...) all-reduce(bf16[1536]{0:T(1024)(128)(2,1)S(1)} %dynamic-update-slic, ...), channel_id=1, replica_groups=mesh['seq'=2,'dp'=16] {'dp'}, use_global_device_ids=true, to_apply=%add | all-reduce | flops 9216 | bytes 36864
  107.8 48.3 %all-to-all-done = bf16[1024,3,2,384]{3,0,1,2:T(8,128)(2,1)} async-done(((bf16[1024,3,2,384]{3,0,1,2:T(8,128)(2,1)}), bf16[1024,3,2,384]{3,0,1,2:T(8,128)(2,1)}, u32[]{:S(2)}, u32[]{:S(2)}) %all-to-all-start) | async-done | bytes 4718624 | tf_op jit(solution)/shard_map/all_to_all | solution.py:104
  173.3 109.2 %while.28 = (s32[]{:T(128)}, bf16[4,512,6,64]{1,3,2,0:T(8,128)(2,1)}, f32[4,6,512,1]{2,1,3,0:T(8,128)}, bf16[4,512,6,64]{1,3,2,0:T(8,128)(2,1)}, bf16[2048,6,64]...) while((s32[]{:T(128)}, bf16[4,512,6,64]{1,3,2,0:T(8,128)(2,1)}, ...), condition=%wide.region_3.4_spmd.clone, body=%wide.region_0.3_spmd.clone.sunk | while | flops 1686307840 | bytes 180229744 | solution.py:134
  188.7 12.5 %fusion.115 = bf16[4,512,6,64]{1,3,2,0:T(8,128)(2,1)} fusion(bf16[4,512,6,64]{1,3,2,0:T(8,128)(2,1)} %get-tuple-element.584, s32[]{:T(128)} %get-tuple-element.583, bf16[2048,6,64]{0,2,1:T(8,128)(2,1)} %get-tuple-element.596, f32[6,512,2048]{2,1,0:T(8,128)} %copy-done, f32[6,512]{1,0:T(8,128)S(1)} %fusion.114, f32[6,512]{1,0:T(8,128)S(1)} %get-tuple-element.562, ...), kind=kOutput, calls=%fused_computation.10.clone.1 | convolution fusion | flops 836960256 | bytes 27165184 | tf_op jit(solution)/shard_map/while/body/eval_jaxpr/hqk,khe->qhe/dot_general | solution.py:126
  216.0 12.3 %fusion.115 = bf16[4,512,6,64]{1,3,2,0:T(8,128)(2,1)} fusion(bf16[4,512,6,64]{1,3,2,0:T(8,128)(2,1)} %get-tuple-element.584, s32[]{:T(128)} %get-tuple-element.583, bf16[2048,6,64]{0,2,1:T(8,128)(2,1)} %get-tuple-element.596, f32[6,512,2048]{2,1,0:T(8,128)} %copy-done, f32[6,512]{1,0:T(8,128)S(1)} %fusion.114, f32[6,512]{1,0:T(8,128)S(1)} %get-tuple-element.562, ...), kind=kOutput, calls=%fused_computation.10.clone.1 | convolution fusion | flops 836960256 | bytes 27165184 | tf_op jit(solution)/shard_map/while/body/eval_jaxpr/hqk,khe->qhe/dot_general | solution.py:126
  270.1 12.3 %fusion.115 = bf16[4,512,6,64]{1,3,2,0:T(8,128)(2,1)} fusion(bf16[4,512,6,64]{1,3,2,0:T(8,128)(2,1)} %get-tuple-element.584, s32[]{:T(128)} %get-tuple-element.583, bf16[2048,6,64]{0,2,1:T(8,128)(2,1)} %get-tuple-element.596, f32[6,512,2048]{2,1,0:T(8,128)} %copy-done, f32[6,512]{1,0:T(8,128)S(1)} %fusion.114, f32[6,512]{1,0:T(8,128)S(1)} %get-tuple-element.562, ...), kind=kOutput, calls=%fused_computation.10.clone.1 | convolution fusion | flops 836960256 | bytes 27165184 | tf_op jit(solution)/shard_map/while/body/eval_jaxpr/hqk,khe->qhe/dot_general | solution.py:126
  322.9 13.6 %multiply_convert_fusion.1 = (bf16[1024,3072]{1,0:T(8,128)(2,1)}, f32[1024,3072]{1,0:T(8,128)}) fusion(f32[3072]{0:T(1024)S(1)} %convert_element_type.174, bf16[768,3072]{1,0:T(8,128)(2,1)} %all-gather.10.cloned.1.call-done, f32[1024,768]{0,1:T(8,128)} %copy-done.9, f32[768]{0:T(1024)S(1)} %convert_element_type.172, f32[768]{0:T(1024)S(1)} %convert_element_type.171, ...), kind=kOutput, calls=%fused_computation.49 | convolution fusion | flops 4854644736 | bytes 26765312 | tf_op jit(solution)/shard_map/dot_general | solution.py:23
  352.4 15.8 %convert_reduce_fusion = (f32[3072]{0:T(1024)}, bf16[1024,3072]{1,0:T(8,128)(2,1)S(1)}) fusion(bf16[1024,768]{0,1:T(8,128)(2,1)S(1)} %get-tuple-element.433, bf16[3072,768]{1,0:T(8,128)(2,1)S(1)} %bitcast.201, f32[1024,3072]{1,0:T(8,128)} %get-tuple-element.457, f32[3072]{0:T(1024)S(1)} %convert_element_type.174), kind=kOutput, calls=%fused_computation.47 | convolution fusion | flops 4882166784 | bytes 25190400 | tf_op jit(solution)/shard_map/dot_general | solution.py:33
  425.7 341.1 %while.29 = (s32[]{:T(128)}, f32[2048,6,64]{0,2,1:T(8,128)}, f32[2048,6,64]{0,2,1:T(8,128)}, bf16[4,512,6,64]{1,3,2,0:T(8,128)(2,1)}, bf16[4,512,6,64]{1,3,2,0:T...) while((s32[]{:T(128)}, f32[2048,6,64]{0,2,1:T(8,128)}, ...), condition=%wide.region_14.15_spmd.clone, body=%wide.region_12.14_spmd.clone.sunk | while | flops 4125033472 | bytes 208525968 | solution.py:195
  438.4 16.8 %multiply_reduce_fusion.6 = (f32[6,512]{1,0:T(8,128)S(1)}, f32[6,512,2048]{2,1,0:T(8,128)}) fusion(f32[6,512,2048]{2,1,0:T(8,128)} %fusion.125, f32[6,512]{1,0:T(8,128)S(1)} %dynamic-slice_bitcast_fusion.2, f32[2048]{0:T(1024)S(1)} %fusion.126, bf16[2048,6,64]{0,2,1:T(8,128)(2,1)S(1)} %get-tuple-element.631, ...), kind=kOutput, calls=%fused_computation.20.clone.1 | convolution fusion | flops 836760576 | bytes 52331008 | tf_op jit(solution)/shard_map/while/body/eval_jaxpr/qhe,khe->hqk/dot_general | solution.py:176
  455.2 25.6 %multiply_convert_fusion.3 = bf16[6,512,2048]{2,1,0:T(8,128)(2,1)} fusion(f32[6,512,2048]{2,1,0:T(8,128)} %get-tuple-element.573, f32[6,512,2048]{2,1,0:T(8,128)} %fusion.125, f32[6,512]{1,0:T(8,128)S(1)} %get-tuple-element.574, f32[6,512]{1,0:T(8,128)S(1)} %dynamic-slice_bitcast_fusion.2, f32[2048]{0:T(1024)S(1)} %fusion.126), kind=kLoop, calls=%fused_computation.19.clone.1 | loop fusion | flops 37748736 | bytes 62947328 | tf_op jit(solution)/shard_map/while/body/eval_jaxpr/convert_element_type | solution.py:180
  498.8 12.6 %bitcast_add_fusion.5 = f32[2048,6,64]{0,2,1:T(8,128)} fusion(f32[2048,6,64]{0,2,1:T(8,128)} %get-tuple-element.613, f32[6,512,2048]{2,1,0:T(8,128)} %fusion.125, f32[6,512]{1,0:T(8,128)S(1)} %dynamic-slice_bitcast_fusion.2, f32[2048]{0:T(1024)S(1)} %fusion.126, pred[]{:T(512)S(6)} %compare.3, bf16[4,512,6,64]{1,3,2,0:T(8,128)(2,1)} %get-tuple-element.630, ...), kind=kOutput, calls=%fused_computation.24.clone.1 | convolution fusion | flops 832045056 | bytes 31871488 | tf_op jit(solution)/shard_map/while/body/eval_jaxpr/hqk,qhe->khe/dot_general | solution.py:173
  524.1 17.0 %multiply_reduce_fusion.6 = (f32[6,512]{1,0:T(8,128)S(1)}, f32[6,512,2048]{2,1,0:T(8,128)}) fusion(f32[6,512,2048]{2,1,0:T(8,128)} %fusion.125, f32[6,512]{1,0:T(8,128)S(1)} %dynamic-slice_bitcast_fusion.2, f32[2048]{0:T(1024)S(1)} %fusion.126, bf16[2048,6,64]{0,2,1:T(8,128)(2,1)S(1)} %get-tuple-element.631, ...), kind=kOutput, calls=%fused_computation.20.clone.1 | convolution fusion | flops 836760576 | bytes 52331008 | tf_op jit(solution)/shard_map/while/body/eval_jaxpr/qhe,khe->hqk/dot_general | solution.py:176
  541.2 22.3 %multiply_convert_fusion.3 = bf16[6,512,2048]{2,1,0:T(8,128)(2,1)} fusion(f32[6,512,2048]{2,1,0:T(8,128)} %get-tuple-element.573, f32[6,512,2048]{2,1,0:T(8,128)} %fusion.125, f32[6,512]{1,0:T(8,128)S(1)} %get-tuple-element.574, f32[6,512]{1,0:T(8,128)S(1)} %dynamic-slice_bitcast_fusion.2, f32[2048]{0:T(1024)S(1)} %fusion.126), kind=kLoop, calls=%fused_computation.19.clone.1 | loop fusion | flops 37748736 | bytes 62947328 | tf_op jit(solution)/shard_map/while/body/eval_jaxpr/convert_element_type | solution.py:180
  583.5 15.8 %bitcast_add_fusion.5 = f32[2048,6,64]{0,2,1:T(8,128)} fusion(f32[2048,6,64]{0,2,1:T(8,128)} %get-tuple-element.613, f32[6,512,2048]{2,1,0:T(8,128)} %fusion.125, f32[6,512]{1,0:T(8,128)S(1)} %dynamic-slice_bitcast_fusion.2, f32[2048]{0:T(1024)S(1)} %fusion.126, pred[]{:T(512)S(6)} %compare.3, bf16[4,512,6,64]{1,3,2,0:T(8,128)(2,1)} %get-tuple-element.630, ...), kind=kOutput, calls=%fused_computation.24.clone.1 | convolution fusion | flops 832045056 | bytes 31871488 | tf_op jit(solution)/shard_map/while/body/eval_jaxpr/hqk,qhe->khe/dot_general | solution.py:173
  611.9 17.0 %multiply_reduce_fusion.6 = (f32[6,512]{1,0:T(8,128)S(1)}, f32[6,512,2048]{2,1,0:T(8,128)}) fusion(f32[6,512,2048]{2,1,0:T(8,128)} %fusion.125, f32[6,512]{1,0:T(8,128)S(1)} %dynamic-slice_bitcast_fusion.2, f32[2048]{0:T(1024)S(1)} %fusion.126, bf16[2048,6,64]{0,2,1:T(8,128)(2,1)S(1)} %get-tuple-element.631, ...), kind=kOutput, calls=%fused_computation.20.clone.1 | convolution fusion | flops 836760576 | bytes 52331008 | tf_op jit(solution)/shard_map/while/body/eval_jaxpr/qhe,khe->hqk/dot_general | solution.py:176
  628.9 21.8 %multiply_convert_fusion.3 = bf16[6,512,2048]{2,1,0:T(8,128)(2,1)} fusion(f32[6,512,2048]{2,1,0:T(8,128)} %get-tuple-element.573, f32[6,512,2048]{2,1,0:T(8,128)} %fusion.125, f32[6,512]{1,0:T(8,128)S(1)} %get-tuple-element.574, f32[6,512]{1,0:T(8,128)S(1)} %dynamic-slice_bitcast_fusion.2, f32[2048]{0:T(1024)S(1)} %fusion.126), kind=kLoop, calls=%fused_computation.19.clone.1 | loop fusion | flops 37748736 | bytes 62947328 | tf_op jit(solution)/shard_map/while/body/eval_jaxpr/convert_element_type | solution.py:180
  669.6 14.0 %bitcast_add_fusion.5 = f32[2048,6,64]{0,2,1:T(8,128)} fusion(f32[2048,6,64]{0,2,1:T(8,128)} %get-tuple-element.613, f32[6,512,2048]{2,1,0:T(8,128)} %fusion.125, f32[6,512]{1,0:T(8,128)S(1)} %dynamic-slice_bitcast_fusion.2, f32[2048]{0:T(1024)S(1)} %fusion.126, pred[]{:T(512)S(6)} %compare.3, bf16[4,512,6,64]{1,3,2,0:T(8,128)(2,1)} %get-tuple-element.630, ...), kind=kOutput, calls=%fused_computation.24.clone.1 | convolution fusion | flops 832045056 | bytes 31871488 | tf_op jit(solution)/shard_map/while/body/eval_jaxpr/hqk,qhe->khe/dot_general | solution.py:173
  696.1 16.7 %multiply_reduce_fusion.6 = (f32[6,512]{1,0:T(8,128)S(1)}, f32[6,512,2048]{2,1,0:T(8,128)}) fusion(f32[6,512,2048]{2,1,0:T(8,128)} %fusion.125, f32[6,512]{1,0:T(8,128)S(1)} %dynamic-slice_bitcast_fusion.2, f32[2048]{0:T(1024)S(1)} %fusion.126, bf16[2048,6,64]{0,2,1:T(8,128)(2,1)S(1)} %get-tuple-element.631, ...), kind=kOutput, calls=%fused_computation.20.clone.1 | convolution fusion | flops 836760576 | bytes 52331008 | tf_op jit(solution)/shard_map/while/body/eval_jaxpr/qhe,khe->hqk/dot_general | solution.py:176
  712.8 21.4 %multiply_convert_fusion.3 = bf16[6,512,2048]{2,1,0:T(8,128)(2,1)} fusion(f32[6,512,2048]{2,1,0:T(8,128)} %get-tuple-element.573, f32[6,512,2048]{2,1,0:T(8,128)} %fusion.125, f32[6,512]{1,0:T(8,128)S(1)} %get-tuple-element.574, f32[6,512]{1,0:T(8,128)S(1)} %dynamic-slice_bitcast_fusion.2, f32[2048]{0:T(1024)S(1)} %fusion.126), kind=kLoop, calls=%fused_computation.19.clone.1 | loop fusion | flops 37748736 | bytes 62947328 | tf_op jit(solution)/shard_map/while/body/eval_jaxpr/convert_element_type | solution.py:180
  753.0 13.7 %bitcast_add_fusion.5 = f32[2048,6,64]{0,2,1:T(8,128)} fusion(f32[2048,6,64]{0,2,1:T(8,128)} %get-tuple-element.613, f32[6,512,2048]{2,1,0:T(8,128)} %fusion.125, f32[6,512]{1,0:T(8,128)S(1)} %dynamic-slice_bitcast_fusion.2, f32[2048]{0:T(1024)S(1)} %fusion.126, pred[]{:T(512)S(6)} %compare.3, bf16[4,512,6,64]{1,3,2,0:T(8,128)(2,1)} %get-tuple-element.630, ...), kind=kOutput, calls=%fused_computation.24.clone.1 | convolution fusion | flops 832045056 | bytes 31871488 | tf_op jit(solution)/shard_map/while/body/eval_jaxpr/hqk,qhe->khe/dot_general | solution.py:173
  789.8 67.0 %all_to_all.63 = bf16[2048,3,1,384]{3,1,2,0:T(4,128)(2,1)S(1)} all-to-all(bf16[2048,3,1,384]{3,1,2,0:T(4,128)(2,1)} %copy.174), channel_id=1, replica_groups=mesh['seq'=2,'dp'=16] {'seq'}, dimensions={0} | all-to-all | bytes 9437184 | tf_op jit(solution)/shard_map/all_to_all | solution.py:207
  905.0 79.5 %all-reduce.16 = (bf16[1536]{0:T(1024)(128)(2,1)S(1)}, bf16[768]{0:T(1024)(128)(2,1)S(1)}, bf16[3072]{0:T(1024)(128)(2,1)S(1)}, bf16[768]{0:T(1024)(128)(2,1)S(1...) all-reduce(f32[1536]{0:T(1024)S(1)} %pad_maximum_fusion.2, ...), channel_id=4, replica_groups=mesh['seq'=2,'dp'=16] {'dp'}, use_global_device_ids=true, to_apply=%region_18.19.clone | all-reduce | flops 9216 | bytes 55296
  1009.5 16.4 %all-reduce.22.cloned.1.call-done = (bf16[48,768]{1,0:T(8,128)(2,1)}, bf16[48,3072]{1,0:T(8,128)(2,1)}, bf16[192,768]{1,0:T(8,128)(2,1)}) async-done(((bf16[48,768]{1,0:T(8,128)(2,1)}, bf16[48,3072]{1,0:T(8,128)(2,1)}, bf16[192,768]{1,0:T(8,128)(2,1)}), (bf16[48,768]{1,0:T(8,128)(2,1)}, bf16[48,3072]{1,0:T(8,128)(2,1)}, bf16[192,768]{1,0:T(8,128)(2,1)})) %all-reduce.22.cloned.1.call-update) | async-done | bytes 663568 | tf_op jit(solution)/shard_map/psum | solution.py:245
  (284 shorter events, 462.8 us)
Async XLA Ops:
  7.2 76.1 %all-gather.6.cloned.1.call-start = ((), (), s32[]{:S(2)}) async-start(), calls=%async_computation.8 | async-start | bytes 3760128 | tf_op jit(solution)/shard_map/all_gather | solution.py:81
  7.9 309.0 %all-gather.8.cloned.1.call-start = ((), (), s32[]{:S(2)}) async-start(), calls=%async_computation.9 | async-start | bytes 1253376 | tf_op jit(solution)/shard_map/all_gather | solution.py:83
  8.7 314.2 %all-gather.10.cloned.1.call-start = ((), (), s32[]{:S(2)}) async-start(), calls=%async_computation.10 | async-start | bytes 5013504 | tf_op jit(solution)/shard_map/all_gather | solution.py:85
  101.4 54.7 %all-to-all-start = ((bf16[1024,3,2,384]{3,0,1,2:T(8,128)(2,1)}), bf16[1024,3,2,384]{3,0,1,2:T(8,128)(2,1)}, u32[]{:S(2)}, u32[]{:S(2)}) async-start(bf16[1024,3,2,384]{3,0,1,2:T(8,128)(2,1)} %copy.159), calls=%async_computation | async-start | bytes 9437184 | tf_op jit(solution)/shard_map/all_to_all | solution.py:104
  107.2 229.3 %all-gather.12.cloned.1.call-start = ((), (), s32[]{:S(2)}) async-start(), calls=%async_computation.11 | async-start | bytes 5013504 | tf_op jit(solution)/shard_map/all_gather | solution.py:87
  179.1 8.9 copy-start
  207.0 8.4 copy-start
  234.1 8.3 copy-start
  261.2 8.3 copy-start
  292.6 18.0 %all-to-all-start.1 = ((bf16[2,2,196608]{2,1,0:T(2,128)(2,1)}), bf16[2,2,196608]{2,1,0:T(2,128)(2,1)S(1)}, u32[]{:S(2)}, u32[]{:S(2)}) async-start(bf16[2,2,196608]{2,1,0:T(2,128)(2,1)} %reshape.259), calls=%async_computation.1 | async-start | bytes 3145728 | tf_op jit(solution)/shard_map/all_to_all | solution.py:136
  296.4 600.1 %reduce-scatter.7.cloned.1.call-start = ((), (), s32[]{:S(2)}) async-start(), calls=%async_computation.12 | async-start | bytes 2506752 | tf_op jit(solution)/shard_map/reduce_scatter | solution.py:217
  300.3 67.9 %copy-start.5 = (bf16[1,1024,768]{1,2,0:T(8,128)(2,1)}, bf16[1,1024,768]{1,2,0:T(8,128)(2,1)S(1)}, u32[]{:S(2)}) copy-start(bf16[1,1024,768]{1,2,0:T(8,128)(2,1)S(1)} %copy.168) | copy-start | bytes 4718596
  349.0 19.1 %slice-start = ((s8[4718592]{0:T(1024)(128)(4,1)}), s8[4194304]{0:T(1024)(128)(4,1)S(1)}, s32[]{:S(2)}) async-start(s8[4718592]{0:T(1024)(128)(4,1)} %bitcast.198), calls=%async_computation.17 | async-start | bytes 8388608
  352.3 15.8 %copy-start.17 = (bf16[1024,768]{0,1:T(8,128)(2,1)}, bf16[1024,768]{0,1:T(8,128)(2,1)S(1)}, u32[]{:S(2)}) copy-start(bf16[1024,768]{0,1:T(8,128)(2,1)S(1)} %get-tuple-element.433) | copy-start | bytes 4718596
  352.3 15.8 %copy-start.10 = (f32[1024,768]{0,1:T(8,128)S(1)}, f32[1024,768]{0,1:T(8,128)}, u32[]{:S(2)}) copy-start(f32[1024,768]{0,1:T(8,128)} %copy-done.9) | copy-start | bytes 9437188
  352.4 15.8 %slice-start.1 = ((s8[4718592]{0:T(1024)(128)(4,1)}), s8[524288]{0:T(1024)(128)(4,1)S(1)}, s32[]{:S(2)}) async-start(s8[4718592]{0:T(1024)(128)(4,1)} %bitcast.198), calls=%async_computation.18 | async-start | bytes 1048576
  382.8 515.3 %reduce-scatter.9.cloned.1.call-start = ((), (), s32[]{:S(2)}) async-start(), calls=%async_computation.13 | async-start | bytes 10027008 | tf_op jit(solution)/shard_map/reduce_scatter | solution.py:219
  397.8 17.0 %all-to-all-start.2 = ((bf16[1024,2,384]{0,2,1:T(8,128)(2,1)}), bf16[1024,2,384]{0,2,1:T(8,128)(2,1)S(1)}, u32[]{:S(2)}, u32[]{:S(2)}) async-start(bf16[1024,2,384]{0,2,1:T(8,128)(2,1)} %bitcast.21), calls=%async_computation.2 | async-start | bytes 3145728 | tf_op jit(solution)/shard_map/all_to_all | solution.py:165
  401.6 498.3 %reduce-scatter.11.cloned.1.call-start = ((), (), s32[]{:S(2)}) async-start(), calls=%async_computation.14 | async-start | bytes 10027008 | tf_op jit(solution)/shard_map/reduce_scatter | solution.py:221
  412.2 584.3 %reduce-scatter.13.cloned.1.call-start = ((), (), s32[]{:S(2)}) async-start(), calls=%async_computation.15 | async-start | bytes 7520256 | tf_op jit(solution)/shard_map/reduce_scatter | solution.py:215
  417.6 8.2 copy-start.1
  417.6 8.2 copy-start.4
  882.5 143.4 %all-reduce.22.cloned.1.call-start = ((), (), s32[]{:S(2)}) async-start(), calls=%async_computation.16 | async-start | bytes 1327104 | tf_op jit(solution)/shard_map/psum | solution.py:245
  899.9 94.3 %copy-start.13 = (f32[1,1024,768]{1,2,0:T(8,128)S(1)}, f32[1,1024,768]{1,2,0:T(8,128)}, u32[]{:S(2)}) copy-start(f32[1,1024,768]{1,2,0:T(8,128)} %add_bitcast_fusion) | copy-start | bytes 9437188
  (33 other events, 142.5 us)
Sparse Core Ops, SparseCore 0:
  10.3 50.6 all-gather.5
  63.2 36.8 all-gather.7
  102.4 52.3 all-gather.9
  156.9 51.9 all-gather.11
  382.9 66.6 reduce-scatter.6
  454.1 110.4 reduce-scatter.8
  568.7 111.1 reduce-scatter.10
  882.6 108.0 reduce-scatter.12
  994.3 31.5 all-reduce.21
